TPU v7x, 512 devices: a whole 4x4x16 slice. The times are simulated.
512 devices in a mesh: dp: 4 (over y), frames: 16 (over z), height: 8 (over x, core).
Axes of the slice: x: 4, y: 4, z: 16, core: 2. Of those that a mesh axis runs over, the one named last changes fastest.
Arguments:
- video: bfloat16 [512, 8, 16, 640], P(('dp', 'frames'), 'height'), parts along dimension 0
- window_gaps: int32 [112], P('dp'), parts along dimension 0, may hold values from 1 to 8, 112 in all
- gn_gain: float32 [640], replicated, may hold values from 0.25 to 1.75
- gn_bias: float32 [640], replicated, may hold values from -3 to 3
- conv_weight: bfloat16 [5760, 640], P('frames', 'height'), may hold values from -0.078125 to 0.078125
- conv_bias: float32 [640], replicated, may hold values from -3 to 3
- ln_gain: float32 [640], replicated, may hold values from 0.25 to 1.75
- ln_bias: float32 [640], replicated, may hold values from -3 to 3
- qkv_weight: bfloat16 [640, 1920], replicated, may hold values from -0.25 to 0.25
- out_weight: bfloat16 [640, 640], replicated, may hold values from -0.5 to 0.5
- out_bias: float32 [640], replicated, may hold values from -3 to 3
Outputs:
- output: bfloat16 [512, 8, 16, 640], P(('dp', 'frames'), 'height'), parts along dimension 0
There are 4 independent parts, one for each index of `dp`. A program takes and returns all parts, laid end to end along the dimension named above; an argument that names none is the same for every part. Nothing has to cross between parts.
Inputs may be any that keep to these rules, and one draw needn't show every extreme that they name: `window_gaps`: the first window starts at frame 0 and the last at 112; the largest gap 16 // 2 is reached in every draw.
All inputs are finite; a program needn't handle non-finite values.
Results may differ from a plain program's by a relative error of at most 0.008.
Values may be sent and summed in bfloat16 or wider, within the bound.
No kernel may reach another device: no remote copies, remote signals or barrier semaphores. Data moves between devices by JAX's collectives and lax.ppermute only.
A program may use at most 64 MiB of HBM per device.

v0:
```python
import jax
import jax.numpy as jnp
from jax import lax
from jax.sharding import PartitionSpec as P

HEADS = 10
GROUPS = 32
WIN = 16
HEAD_DIM = 64
EPSILON = 1e-05


def passed_along(shard, axis, by):
    size = lax.axis_size(axis)
    pairs = [(i, i + by) for i in range(size) if 0 <= i + by < size]
    return lax.ppermute(shard, axis, pairs)


def extended_2(cells, sides, width):
    for axis, dim in sides:
        count = lax.axis_size(axis)
        ends = count - 1
        head = lax.slice_in_dim(cells, 0, width, axis=dim)
        tail = lax.slice_in_dim(cells, cells.shape[dim] - width, cells.shape[dim], axis=dim)
        cells = jnp.concatenate(
            [
                lax.ppermute(tail, axis, [(i, (i + 1) % count) for i in range(ends)]),
                cells,
                lax.ppermute(head, axis, [((i + 1) % count, i) for i in range(ends)]),
            ],
            axis=dim,
        )
    return cells


def fetch_neighbour(keys, values, offset):
    return passed_along((keys, values), "frames", offset)


def window_starts(window_gaps):
    return jnp.concatenate([jnp.zeros((1,), jnp.int32), jnp.cumsum(window_gaps)])


def on_device(
    video,
    window_gaps,
    gn_gain,
    gn_bias,
    conv_weight,
    conv_bias,
    ln_gain,
    ln_bias,
    qkv_weight,
    out_weight,
    out_bias,
):
    frames_dev, rows_dev, width, chans = video.shape
    bands = lax.axis_size("height")
    floats = video.astype(jnp.float32)
    grouped = floats.reshape(frames_dev, rows_dev, width, GROUPS, chans // GROUPS)
    cell_count = rows_dev * bands * width * (chans // GROUPS)
    mean = lax.psum(jnp.sum(grouped, axis=(1, 2, 4)), "height") / cell_count
    centred = grouped - mean[:, None, None, :, None]
    variance = lax.psum(jnp.sum(centred * centred, axis=(1, 2, 4)), "height") / cell_count
    scaled = (grouped - mean[:, None, None, :, None]) * lax.rsqrt(variance + EPSILON)[
        :, None, None, :, None
    ]
    normed = scaled.reshape(floats.shape) * gn_gain + gn_bias
    activated = jax.nn.silu(normed).astype(jnp.bfloat16)
    columns = lax.all_gather(conv_weight, "height", axis=1, tiled=True)
    extended = extended_2(activated, (("height", 1),), 1)
    extended = jnp.pad(extended, ((0, 0), (0, 0), (1, 1), (0, 0)))
    patches = jnp.concatenate(
        [
            extended[:, row_off : row_off + rows_dev, col_off : col_off + width]
            for row_off in range(3)
            for col_off in range(3)
        ],
        axis=3,
    ).reshape(-1, 9 * chans)
    conv_sum = jnp.dot(
        patches,
        lax.all_gather(columns, "frames", axis=0, tiled=True),
        preferred_element_type=jnp.float32,
    )
    conv_out = (
        (conv_sum + conv_bias).astype(jnp.bfloat16).reshape(frames_dev, rows_dev, width, chans)
    )
    conv_out = lax.optimization_barrier(conv_out)
    resid_state = (floats + conv_out.astype(jnp.float32)).astype(jnp.bfloat16)
    resid_float = resid_state.astype(jnp.float32)
    centre = jnp.mean(resid_float, axis=-1, keepdims=True)
    deviation = resid_float - centre
    spread = jnp.mean(deviation * deviation, axis=-1, keepdims=True)
    normalized = (deviation * lax.rsqrt(spread + EPSILON) * ln_gain + ln_bias).astype(jnp.bfloat16)
    cells = rows_dev * width
    project = jnp.dot(
        normalized.reshape(-1, chans), qkv_weight, preferred_element_type=jnp.float32
    ).astype(jnp.bfloat16)
    scale = HEAD_DIM ** (-0.5)
    starts = window_starts(window_gaps)
    project = project.reshape(frames_dev, cells, 3 * chans)
    query = project[:, :, :chans]
    keys = project[:, :, chans : 2 * chans]
    values = project[:, :, 2 * chans :]
    gathered = [fetch_neighbour(keys, values, offset) for offset in (2, 1)]
    gathered.append((keys, values))
    gathered = gathered + [fetch_neighbour(keys, values, offset) for offset in (-1, -2)]
    keys_near = jnp.concatenate([pair[0] for pair in gathered], axis=0).reshape(
        -1, cells, HEADS, HEAD_DIM
    )
    values_near = jnp.concatenate([pair[1] for pair in gathered], axis=0).reshape(
        -1, cells, HEADS, HEAD_DIM
    )
    near_ids = (lax.axis_index("frames") - 2) * frames_dev + jnp.arange(
        5 * frames_dev, dtype=jnp.int32
    )
    inside = (near_ids[None, :] >= starts[:, None]) & (near_ids[None, :] < starts[:, None] + WIN)
    member = inside.astype(jnp.float32)
    cover = member[:, 2 * frames_dev : 3 * frames_dev].T
    frame_count = jnp.sum(cover, axis=1)
    scores = (
        jnp.einsum(
            "nshd,mshd->shnm",
            query.reshape(frames_dev, cells, HEADS, HEAD_DIM),
            keys_near,
            preferred_element_type=jnp.float32,
        )
        * scale
    )
    expo = jnp.exp(scores)
    window_sum = jnp.einsum("shnm,wm->shnw", expo, member, precision=lax.Precision.HIGHEST)
    coef = cover / (frame_count[:, None] * jnp.where(cover > 0, window_sum, 1.0))
    spread_back = jnp.einsum("shnw,wm->shnm", coef, member, precision=lax.Precision.HIGHEST)
    attn_weight = (expo * spread_back).astype(jnp.bfloat16)
    mixed = (
        jnp.einsum("shnm,mshd->nshd", attn_weight, values_near, preferred_element_type=jnp.float32)
        .astype(jnp.bfloat16)
        .reshape(-1, chans)
    )
    projected = jnp.dot(mixed, out_weight, preferred_element_type=jnp.float32)
    output = resid_float.reshape(-1, chans) + projected + out_bias
    return output.astype(jnp.bfloat16).reshape(frames_dev, rows_dev, width, chans)


def solution(mesh):
    placed = (
        P(("dp", "frames"), "height", None, None),
        P("dp"),
        P(),
        P(),
        P("frames", "height"),
        P(),
        P(),
        P(),
        P(),
        P(),
        P(),
    )
    return jax.shard_map(
        on_device,
        mesh=mesh,
        in_specs=placed,
        out_specs=P(("dp", "frames"), "height", None, None),
        check_vma=False,
    )
```

profile of v0, /device:TPU:2, one launch (start us, length us, event | category | flops | bytes accessed | tf_op | source)
XLA Modules:
  0.0 188.5 jit_solution(935710017307930549)
XLA Ops:
  6.5 16.2 %all_gather.6 = bf16[360,640]{0,1:T(8,128)(2,1)S(1)} all-gather(bf16[360,80]{0,1:T(8,128)(2,1)} %param.15), channel_id=1, replica_groups=mesh['dp'=4,'frames'=16,'height'=8] {'height'}, dimensions={1}, use_global_device_ids=true | all-gather | bytes 518400 | tf_op jit(solution)/shard_map/all_gather | solution.py:70
  22.7 1.0 copy.46
  24.2 13.0 %psum.14 = f32[8,32]{1,0:T(8,128)S(1)} all-reduce(f32[8,32]{1,0:T(8,128)S(1)} %reduce_sum.61), channel_id=1, replica_groups=mesh['dp'=4,'frames'=16,'height'=8] {'height'}, use_global_device_ids=true, to_apply=%region_2.0 | all-reduce | flops 256 | bytes 2048 | tf_op jit(solution)/shard_map/psum | solution.py:62
  37.8 12.3 %psum.15 = f32[8,32]{1,0:T(8,128)S(1)} all-reduce(f32[8,32]{1,0:T(8,128)S(1)} %reduce_sum.64), channel_id=1, replica_groups=mesh['dp'=4,'frames'=16,'height'=8] {'height'}, use_global_device_ids=true, to_apply=%region_5.6 | all-reduce | flops 256 | bytes 2048 | tf_op jit(solution)/shard_map/psum | solution.py:64
  50.5 1.9 %collective-permute-start = (bf16[8,1,16,640]{3,2,1,0:T(8,128)(2,1)S(1)}, bf16[8,1,16,640]{3,2,1,0:T(8,128)(2,1)S(1)}, u32[]{:S(2)}, u32[]{:S(2)}) collective-permute-start(bf16[8,1,16,640]{3,2,1,0:T(8,128)(2,1)S(1)} %fusion.38), channel_id=1, source_target_pairs={{0,1},{1,2},{2,3},{3,4},{4,5},{5,6},{6,7},{8,9},{9,10},{10,11},{11... | collective-permute-start | bytes 491528 | tf_op jit(solution)/shard_map/ppermute | solution.py:27
  52.4 4.7 %collective-permute-start.1 = (bf16[8,1,16,640]{3,2,1,0:T(8,128)(2,1)S(1)}, bf16[8,1,16,640]{3,2,1,0:T(8,128)(2,1)S(1)}, u32[]{:S(2)}, u32[]{:S(2)}) collective-permute-start(bf16[8,1,16,640]{3,2,1,0:T(8,128)(2,1)S(1)} %fusion.38), channel_id=1, source_target_pairs={{1,0},{2,1},{3,2},{4,3},{5,4},{6,5},{7,6},{9,8},{10,9},{11,10},{12... | collective-permute-start | bytes 491528 | tf_op jit(solution)/shard_map/ppermute | solution.py:29
  58.2 1.8 collective-permute-done.1
  66.7 54.3 %all-gather.2.cloned.1.call-done = bf16[5760,640]{1,0:T(8,128)(2,1)} async-done(((bf16[360,640]{1,0:T(8,128)(2,1)}), bf16[5760,640]{1,0:T(8,128)(2,1)}) %all-gather.2.cloned.1.call-update) | async-done | bytes 7372816 | tf_op jit(solution)/shard_map/all_gather | solution.py:83
  121.0 4.9 %fusion.21 = bf16[128,640]{1,0:T(8,128)(2,1)S(1)} fusion(bf16[128,5760]{1,0:T(8,128)(2,1)} %bitcast, bf16[5760,640]{1,0:T(8,128)(2,1)} %all-gather.2.cloned.1.call-done, f32[640]{0:T(1024)S(1)} %copy-done.6), kind=kOutput, calls=%fused_computation.20 | convolution fusion | flops 943882240 | bytes 9013760 | tf_op jit(solution)/shard_map/dot_general | solution.py:81
  127.1 2.7 %collective-permute-start.6 = (bf16[8,16,640]{2,1,0:T(8,128)(2,1)S(1)}, bf16[8,16,640]{2,1,0:T(8,128)(2,1)S(1)}, u32[]{:S(2)}, u32[]{:S(2)}) collective-permute-start(bf16[8,16,640]{2,1,0:T(8,128)(2,1)S(1)} %get-tuple-element.11), channel_id=1, source_target_pairs={{0,16},{8,24},{16,32},{24,40},{32,48},{40,56},{48,64},{56,72},{64,... | collective-permute-start | bytes 491528 | tf_op jit(solution)/shard_map/ppermute | solution.py:16
  129.8 4.9 %collective-permute-start.2 = (bf16[8,16,640]{2,1,0:T(8,128)(2,1)S(1)}, bf16[8,16,640]{2,1,0:T(8,128)(2,1)S(1)}, u32[]{:S(2)}, u32[]{:S(2)}) collective-permute-start(bf16[8,16,640]{2,1,0:T(8,128)(2,1)S(1)} %get-tuple-element.10), channel_id=1, source_target_pairs={{0,16},{8,24},{16,32},{24,40},{32,48},{40,56},{48,64},{56,72},{64,... | collective-permute-start | bytes 491528 | tf_op jit(solution)/shard_map/ppermute | solution.py:16
  134.8 3.8 %collective-permute-start.7 = (bf16[8,16,640]{2,1,0:T(8,128)(2,1)S(1)}, bf16[8,16,640]{2,1,0:T(8,128)(2,1)S(1)}, u32[]{:S(2)}, u32[]{:S(2)}) collective-permute-start(bf16[8,16,640]{2,1,0:T(8,128)(2,1)S(1)} %get-tuple-element.11), channel_id=1, source_target_pairs={{0,8},{8,16},{16,24},{24,32},{32,40},{40,48},{48,56},{56,64},{64,7... | collective-permute-start | bytes 491528 | tf_op jit(solution)/shard_map/ppermute | solution.py:16
  138.6 3.8 %collective-permute-start.3 = (bf16[8,16,640]{2,1,0:T(8,128)(2,1)S(1)}, bf16[8,16,640]{2,1,0:T(8,128)(2,1)S(1)}, u32[]{:S(2)}, u32[]{:S(2)}) collective-permute-start(bf16[8,16,640]{2,1,0:T(8,128)(2,1)S(1)} %get-tuple-element.10), channel_id=1, source_target_pairs={{0,8},{8,16},{16,24},{24,32},{32,40},{40,48},{48,56},{56,64},{64,7... | collective-permute-start | bytes 491528 | tf_op jit(solution)/shard_map/ppermute | solution.py:16
  142.4 1.3 collective-permute-start.4
  143.7 1.3 collective-permute-start.5
  145.0 1.3 collective-permute-start.8
  147.0 1.3 collective-permute-start.9
  152.2 7.9 %collective-permute-done.5 = bf16[8,16,640]{2,1,0:T(8,128)(2,1)S(1)} collective-permute-done((bf16[8,16,640]{2,1,0:T(8,128)(2,1)S(1)}, bf16[8,16,640]{2,1,0:T(8,128)(2,1)S(1)}, u32[]{:S(2)}, u32[]{:S(2)}) %collective-permute-start.5) | collective-permute-done | bytes 163872 | tf_op jit(solution)/shard_map/ppermute | solution.py:16
  160.8 4.1 %reshape.144 = bf16[40,16,10,64]{3,2,1,0:T(8,128)(2,1)} reshape(bf16[40,16,640]{2,1,0:T(8,128)(2,1)} %constant_dynamic-update-slice_fusion.3) | data formatting | bytes 1638400 | tf_op jit(solution)/shard_map/reshape | solution.py:112
  165.6 2.7 %collective-permute-done.9 = bf16[8,16,640]{2,1,0:T(8,128)(2,1)S(1)} collective-permute-done((bf16[8,16,640]{2,1,0:T(8,128)(2,1)S(1)}, bf16[8,16,640]{2,1,0:T(8,128)(2,1)S(1)}, u32[]{:S(2)}, u32[]{:S(2)}) %collective-permute-start.9) | collective-permute-done | bytes 163872 | tf_op jit(solution)/shard_map/ppermute | solution.py:16
  168.9 4.1 %reshape.146 = bf16[40,16,10,64]{3,2,1,0:T(8,128)(2,1)} reshape(bf16[40,16,640]{2,1,0:T(8,128)(2,1)} %constant_dynamic-update-slice_fusion.8) | data formatting | bytes 1638400 | tf_op jit(solution)/shard_map/reshape | solution.py:109
  173.3 3.0 %fusion.8 = f32[16,10,8,40]{3,2,1,0:T(8,128)S(1)} fusion(bf16[40,16,10,64]{3,2,1,0:T(8,128)(2,1)} %reshape.146, bf16[8,16,10,64]{3,2,1,0:T(8,128)(2,1)S(1)} %reshape.145), kind=kOutput, calls=%fused_computation.10 | convolution fusion | flops 6604800 | bytes 1187840 | tf_op jit(solution)/shard_map/nshd,mshd->shnm/dot_general | solution.py:123
  178.0 1.0 fusion.18
  179.5 2.1 %fusion.22 = bf16[128,640]{1,0:T(8,128)(2,1)} fusion(bf16[128,640]{1,0:T(8,128)(2,1)S(1)} %reshape.149, bf16[640,640]{1,0:T(8,128)(2,1)} %param.20, f32[640]{0:T(1024)S(1)} %copy-done.9, bf16[128,640]{1,0:T(8,128)(2,1)S(1)} %bitcast.36), kind=kOutput, calls=%fused_computation.21 | convolution fusion | flops 105185280 | bytes 1313280 | tf_op jit(solution)/shard_map/dot_general | solution.py:141
  (84 shorter events, 19.3 us)
Async XLA Ops:
  6.5 119.9 %copy-start = (bf16[640,1920]{1,0:T(8,128)(2,1)S(1)}, bf16[640,1920]{1,0:T(8,128)(2,1)}, u32[]{:S(2)}) copy-start(bf16[640,1920]{1,0:T(8,128)(2,1)} %param.19) | copy-start | bytes 7372804
  6.5 17.3 %copy-start.1 = (bf16[8,1,16,640]{3,2,1,0:T(8,128)(2,1)S(1)}, bf16[8,1,16,640]{3,2,1,0:T(8,128)(2,1)}, u32[]{:S(2)}) copy-start(bf16[8,1,16,640]{3,2,1,0:T(8,128)(2,1)} %param.11) | copy-start | bytes 491524
  6.5 114.5 %all-gather.2.cloned.1.call-start = ((), (), s32[]{:S(2)}) async-start(), calls=%async_computation | async-start | bytes 7833600 | tf_op jit(solution)/shard_map/all_gather | solution.py:83
  22.7 27.6 %copy-start.4 = (f32[640]{0:T(1024)S(1)}, f32[640]{0:T(1024)}, u32[]{:S(2)}) copy-start(f32[640]{0:T(1024)} %param.14) | copy-start | bytes 7684
  22.7 27.6 %copy-start.5 = (f32[640]{0:T(1024)S(1)}, f32[640]{0:T(1024)}, u32[]{:S(2)}) copy-start(f32[640]{0:T(1024)} %param.13) | copy-start | bytes 7684
  22.7 34.4 %copy-start.10 = (s32[28]{0:T(128)S(1)}, s32[28]{0:T(128)}, u32[]{:S(2)}) copy-start(s32[28]{0:T(128)} %param.12) | copy-start | bytes 340
  50.5 7.7 %collective-permute-start = (bf16[8,1,16,640]{3,2,1,0:T(8,128)(2,1)S(1)}, bf16[8,1,16,640]{3,2,1,0:T(8,128)(2,1)S(1)}, u32[]{:S(2)}, u32[]{:S(2)}) collective-permute-start(bf16[8,1,16,640]{3,2,1,0:T(8,128)(2,1)S(1)} %fusion.38), channel_id=1, source_target_pairs={{0,1},{1,2},{2,3},{3,4},{4,5},{5,6},{6,7},{8,9},{9,10},{10,11},{11... | collective-permute-start | bytes 491528 | tf_op jit(solution)/shard_map/ppermute | solution.py:27
  52.4 7.5 %collective-permute-start.1 = (bf16[8,1,16,640]{3,2,1,0:T(8,128)(2,1)S(1)}, bf16[8,1,16,640]{3,2,1,0:T(8,128)(2,1)S(1)}, u32[]{:S(2)}, u32[]{:S(2)}) collective-permute-start(bf16[8,1,16,640]{3,2,1,0:T(8,128)(2,1)S(1)} %fusion.38), channel_id=1, source_target_pairs={{1,0},{2,1},{3,2},{4,3},{5,4},{6,5},{7,6},{9,8},{10,9},{11,10},{12... | collective-permute-start | bytes 491528 | tf_op jit(solution)/shard_map/ppermute | solution.py:29
  60.2 60.8 %copy-start.6 = (f32[640]{0:T(1024)S(1)}, f32[640]{0:T(1024)}, u32[]{:S(2)}) copy-start(f32[640]{0:T(1024)} %param.16) | copy-start | bytes 7684
  121.0 5.3 %copy-start.7 = (f32[640]{0:T(1024)S(1)}, f32[640]{0:T(1024)}, u32[]{:S(2)}) copy-start(f32[640]{0:T(1024)} %param.18) | copy-start | bytes 7684
  121.0 5.3 %copy-start.8 = (f32[640]{0:T(1024)S(1)}, f32[640]{0:T(1024)}, u32[]{:S(2)}) copy-start(f32[640]{0:T(1024)} %param.17) | copy-start | bytes 7684
  127.1 16.6 %collective-permute-start.6 = (bf16[8,16,640]{2,1,0:T(8,128)(2,1)S(1)}, bf16[8,16,640]{2,1,0:T(8,128)(2,1)S(1)}, u32[]{:S(2)}, u32[]{:S(2)}) collective-permute-start(bf16[8,16,640]{2,1,0:T(8,128)(2,1)S(1)} %get-tuple-element.11), channel_id=1, source_target_pairs={{0,16},{8,24},{16,32},{24,40},{32,48},{40,56},{48,64},{56,72},{64,... | collective-permute-start | bytes 491528 | tf_op jit(solution)/shard_map/ppermute | solution.py:16
  129.8 15.2 %collective-permute-start.2 = (bf16[8,16,640]{2,1,0:T(8,128)(2,1)S(1)}, bf16[8,16,640]{2,1,0:T(8,128)(2,1)S(1)}, u32[]{:S(2)}, u32[]{:S(2)}) collective-permute-start(bf16[8,16,640]{2,1,0:T(8,128)(2,1)S(1)} %get-tuple-element.10), channel_id=1, source_target_pairs={{0,16},{8,24},{16,32},{24,40},{32,48},{40,56},{48,64},{56,72},{64,... | collective-permute-start | bytes 491528 | tf_op jit(solution)/shard_map/ppermute | solution.py:16
  134.8 12.2 %collective-permute-start.7 = (bf16[8,16,640]{2,1,0:T(8,128)(2,1)S(1)}, bf16[8,16,640]{2,1,0:T(8,128)(2,1)S(1)}, u32[]{:S(2)}, u32[]{:S(2)}) collective-permute-start(bf16[8,16,640]{2,1,0:T(8,128)(2,1)S(1)} %get-tuple-element.11), channel_id=1, source_target_pairs={{0,8},{8,16},{16,24},{24,32},{32,40},{40,48},{48,56},{56,64},{64,7... | collective-permute-start | bytes 491528 | tf_op jit(solution)/shard_map/ppermute | solution.py:16
  138.6 9.7 %collective-permute-start.3 = (bf16[8,16,640]{2,1,0:T(8,128)(2,1)S(1)}, bf16[8,16,640]{2,1,0:T(8,128)(2,1)S(1)}, u32[]{:S(2)}, u32[]{:S(2)}) collective-permute-start(bf16[8,16,640]{2,1,0:T(8,128)(2,1)S(1)} %get-tuple-element.10), channel_id=1, source_target_pairs={{0,8},{8,16},{16,24},{24,32},{32,40},{40,48},{48,56},{56,64},{64,7... | collective-permute-start | bytes 491528 | tf_op jit(solution)/shard_map/ppermute | solution.py:16
  142.4 9.1 %collective-permute-start.4 = (bf16[8,16,640]{2,1,0:T(8,128)(2,1)S(1)}, bf16[8,16,640]{2,1,0:T(8,128)(2,1)S(1)}, u32[]{:S(2)}, u32[]{:S(2)}) collective-permute-start(bf16[8,16,640]{2,1,0:T(8,128)(2,1)S(1)} %get-tuple-element.10), channel_id=1, source_target_pairs={{8,0},{16,8},{24,16},{32,24},{40,32},{48,40},{56,48},{64,56},{72,6... | collective-permute-start | bytes 491528 | tf_op jit(solution)/shard_map/ppermute | solution.py:16
  143.7 16.5 %collective-permute-start.5 = (bf16[8,16,640]{2,1,0:T(8,128)(2,1)S(1)}, bf16[8,16,640]{2,1,0:T(8,128)(2,1)S(1)}, u32[]{:S(2)}, u32[]{:S(2)}) collective-permute-start(bf16[8,16,640]{2,1,0:T(8,128)(2,1)S(1)} %get-tuple-element.10), channel_id=1, source_target_pairs={{16,0},{24,8},{32,16},{40,24},{48,32},{56,40},{64,48},{72,56},{80,... | collective-permute-start | bytes 491528 | tf_op jit(solution)/shard_map/ppermute | solution.py:16
  145.0 19.9 %collective-permute-start.8 = (bf16[8,16,640]{2,1,0:T(8,128)(2,1)S(1)}, bf16[8,16,640]{2,1,0:T(8,128)(2,1)S(1)}, u32[]{:S(2)}, u32[]{:S(2)}) collective-permute-start(bf16[8,16,640]{2,1,0:T(8,128)(2,1)S(1)} %get-tuple-element.11), channel_id=1, source_target_pairs={{8,0},{16,8},{24,16},{32,24},{40,32},{48,40},{56,48},{64,56},{72,6... | collective-permute-start | bytes 491528 | tf_op jit(solution)/shard_map/ppermute | solution.py:16
  147.0 21.3 %collective-permute-start.9 = (bf16[8,16,640]{2,1,0:T(8,128)(2,1)S(1)}, bf16[8,16,640]{2,1,0:T(8,128)(2,1)S(1)}, u32[]{:S(2)}, u32[]{:S(2)}) collective-permute-start(bf16[8,16,640]{2,1,0:T(8,128)(2,1)S(1)} %get-tuple-element.11), channel_id=1, source_target_pairs={{16,0},{24,8},{32,16},{40,24},{48,32},{56,40},{64,48},{72,56},{80,... | collective-permute-start | bytes 491528 | tf_op jit(solution)/shard_map/ppermute | solution.py:16
  149.7 0.9 copy-start.3
  176.3 1.8 copy-start.2
  178.0 1.5 copy-start.9
Sparse Core Ops, SparseCore 0:
  23.9 97.0 all-gather.1
where the time goes:
time: 189 us; the launch traced here: 188 us
  waiting for transfers between devices  68.2 us (36%)
  blocking collectives  41.6 us (22%)
  starting transfers between devices  26.9 us (14%)
  local copies, waits for them, and re-layouts  23 us (12%)
  between operations  13.8 us (7%)
  matrix products  12.6 us (7%)
  other arithmetic  2.48 us (1%)
    all_gather x1, waiting for transfers between devices, on_device(): lax.all_gather(columns, 'frames', axis=0, tiled=True)  54.3 us
    ppermute x8, starting transfers between devices, passed_along(): return lax.ppermute(shard, axis, pairs)  20.3 us
    all_gather x1, blocking collectives, on_device(): columns = lax.all_gather(conv_weight, 'height', axis=1, tiled=True)  16.2 us
    psum x1, blocking collectives, on_device(): mean = lax.psum(jnp.sum(grouped, axis=(1, 2, 4)), 'height') / cell_count  13 us
    psum x1, blocking collectives, on_device(): lax.psum(jnp.sum(centred * centred, axis=(1, 2, 4)), 'height') / cell_count  12.3 us
    ppermute x8, waiting for transfers between devices, passed_along(): return lax.ppermute(shard, axis, pairs)  11.5 us
    unnamed x36, local copies, waits for them, and re-layouts  10.1 us
    dot_general x1, matrix products, on_device(): jnp.dot(patches, lax.all_gather(columns, 'frames', axis=0, tiled=True), p...  4.9 us
  transfers between devices with their start and end apart: 11, of which 6 were waited for; matrix products, arithmetic and copies ran while one was open for 9% of the time, Pallas kernels for 0%

commit v1 on v0

--- a/solution.py
+++ b/solution.py
@@ -54,6 +54,13 @@
     out_weight,
     out_bias,
 ):
+
+    def prepare_the_words(a0):
+        r_now = tuple((a0 for _ in range(lax.axis_size("frames"))))
+        formed = jnp.stack(r_now, 0)
+        new = lax.all_to_all(formed, "frames", 0, 0)
+        return jnp.concatenate(new, 0)
+
     frames_dev, rows_dev, width, chans = video.shape
     bands = lax.axis_size("height")
     floats = video.astype(jnp.float32)
@@ -78,11 +85,7 @@
         ],
         axis=3,
     ).reshape(-1, 9 * chans)
-    conv_sum = jnp.dot(
-        patches,
-        lax.all_gather(columns, "frames", axis=0, tiled=True),
-        preferred_element_type=jnp.float32,
-    )
+    conv_sum = jnp.dot(patches, prepare_the_words(columns), preferred_element_type=jnp.float32)
     conv_out = (
         (conv_sum + conv_bias).astype(jnp.bfloat16).reshape(frames_dev, rows_dev, width, chans)
     )

time: 189 us -> 416 us (2.20)
  the two profiles are of different devices: /device:TPU:2 before, /device:TPU:16 now
where the time goes in v1:
time: 416 us; the launch traced here: 415 us
  waiting for transfers between devices  290 us (70%)
  blocking collectives  41.9 us (10%)
  starting transfers between devices  39.9 us (10%)
  local copies, waits for them, and re-layouts  27.5 us (7%)
  matrix products  12.6 us (3%)
    all_to_all x1, waiting for transfers between devices, prepare_the_words(): new = lax.all_to_all(formed, 'frames', 0, 0)  278 us
    ppermute x8, starting transfers between devices, passed_along(): return lax.ppermute(shard, axis, pairs)  21.8 us
    all_to_all x1, starting transfers between devices, prepare_the_words(): new = lax.all_to_all(formed, 'frames', 0, 0)  15.4 us
    psum x1, blocking collectives, on_device(): mean = lax.psum(jnp.sum(grouped, axis=(1, 2, 4)), 'height') / cell_count  14.9 us
    all_gather x1, blocking collectives, on_device(): columns = lax.all_gather(conv_weight, 'height', axis=1, tiled=True)  13.8 us
    psum x1, blocking collectives, on_device(): lax.psum(jnp.sum(centred * centred, axis=(1, 2, 4)), 'height') / cell_count  13.2 us
    unnamed x38, local copies, waits for them, and re-layouts  11.3 us
    ppermute x8, waiting for transfers between devices, passed_along(): return lax.ppermute(shard, axis, pairs)  10.8 us
  transfers between devices with their start and end apart: 11, of which 4 were waited for; matrix products, arithmetic and copies ran while one was open for 4% of the time, Pallas kernels for 0%

profile of v1, /device:TPU:16, one launch (start us, length us, event | category | flops | bytes accessed | tf_op | source)
XLA Modules:
  0.0 415.2 jit_solution(3413460457292602808)
XLA Ops:
  0.0 13.8 %all_gather.3 = bf16[360,640]{0,1:T(8,128)(2,1)S(1)} all-gather(bf16[360,80]{0,1:T(8,128)(2,1)} %param.15), channel_id=1, replica_groups=mesh['dp'=4,'frames'=16,'height'=8] {'height'}, dimensions={1}, use_global_device_ids=true | all-gather | bytes 518400 | tf_op jit(solution)/shard_map/all_gather | solution.py:77
  14.0 3.6 stack.2
  17.6 15.4 %all-to-all-start = ((bf16[16,360,640]{2,1,0:T(8,128)(2,1)}), bf16[16,360,640]{2,1,0:T(8,128)(2,1)}, u32[]{:S(2)}, u32[]{:S(2)}) async-start(bf16[16,360,640]{2,1,0:T(8,128)(2,1)} %stack.2), calls=%async_computation | async-start | bytes 14745600 | tf_op jit(solution)/shard_map/all_to_all | solution.py:61
  33.3 14.9 %psum.14 = f32[8,32]{1,0:T(8,128)S(1)} all-reduce(f32[8,32]{1,0:T(8,128)S(1)} %reduce_sum.61), channel_id=1, replica_groups=mesh['dp'=4,'frames'=16,'height'=8] {'height'}, use_global_device_ids=true, to_apply=%region_2.0 | all-reduce | flops 256 | bytes 2048 | tf_op jit(solution)/shard_map/psum | solution.py:69
  48.8 13.2 %psum.15 = f32[8,32]{1,0:T(8,128)S(1)} all-reduce(f32[8,32]{1,0:T(8,128)S(1)} %reduce_sum.64), channel_id=1, replica_groups=mesh['dp'=4,'frames'=16,'height'=8] {'height'}, use_global_device_ids=true, to_apply=%region_5.6 | all-reduce | flops 256 | bytes 2048 | tf_op jit(solution)/shard_map/psum | solution.py:71
  62.4 1.4 collective-permute-start
  63.8 1.3 collective-permute-start.1
  65.7 1.5 collective-permute-done.1
  74.0 278.1 %all-to-all-done = bf16[16,360,640]{2,1,0:T(8,128)(2,1)} async-done(((bf16[16,360,640]{2,1,0:T(8,128)(2,1)}), bf16[16,360,640]{2,1,0:T(8,128)(2,1)}, u32[]{:S(2)}, u32[]{:S(2)}) %all-to-all-start) | async-done | bytes 7372832 | tf_op jit(solution)/shard_map/all_to_all | solution.py:61
  352.1 4.9 %fusion.21 = bf16[128,640]{1,0:T(8,128)(2,1)S(1)} fusion(bf16[128,5760]{1,0:T(8,128)(2,1)} %bitcast, bf16[5760,640]{1,0:T(8,128)(2,1)} %bitcast.1, f32[640]{0:T(1024)S(1)} %copy-done.7), kind=kOutput, calls=%fused_computation.20 | convolution fusion | flops 943882240 | bytes 9013760 | tf_op jit(solution)/shard_map/dot_general | solution.py:88
  358.8 5.1 %collective-permute-start.6 = (bf16[8,16,640]{2,1,0:T(8,128)(2,1)}, bf16[8,16,640]{2,1,0:T(8,128)(2,1)}, u32[]{:S(2)}, u32[]{:S(2)}) collective-permute-start(bf16[8,16,640]{2,1,0:T(8,128)(2,1)} %get-tuple-element.11), channel_id=1, source_target_pairs={{0,16},{8,24},{16,32},{24,40},{32,48},{40,56},{48,64},{56,72},{64,... | collective-permute-start | bytes 491528 | tf_op jit(solution)/shard_map/ppermute | solution.py:16
  364.0 4.5 %collective-permute-start.2 = (bf16[8,16,640]{2,1,0:T(8,128)(2,1)S(1)}, bf16[8,16,640]{2,1,0:T(8,128)(2,1)S(1)}, u32[]{:S(2)}, u32[]{:S(2)}) collective-permute-start(bf16[8,16,640]{2,1,0:T(8,128)(2,1)S(1)} %get-tuple-element.10), channel_id=1, source_target_pairs={{0,16},{8,24},{16,32},{24,40},{32,48},{40,56},{48,64},{56,72},{64,... | collective-permute-start | bytes 491528 | tf_op jit(solution)/shard_map/ppermute | solution.py:16
  368.7 3.5 collective-permute-start.7
  372.3 3.3 collective-permute-start.3
  375.6 1.3 collective-permute-start.4
  376.9 1.3 collective-permute-start.5
  379.2 1.3 collective-permute-start.8
  381.2 1.5 collective-permute-start.9
  385.7 7.7 %collective-permute-done.5 = bf16[8,16,640]{2,1,0:T(8,128)(2,1)S(1)} collective-permute-done((bf16[8,16,640]{2,1,0:T(8,128)(2,1)S(1)}, bf16[8,16,640]{2,1,0:T(8,128)(2,1)S(1)}, u32[]{:S(2)}, u32[]{:S(2)}) %collective-permute-start.5) | collective-permute-done | bytes 163872 | tf_op jit(solution)/shard_map/ppermute | solution.py:16
  394.1 4.2 reshape.150
  399.2 3.0 collective-permute-done.9
  403.1 2.5 reshape.152
  406.9 3.0 fusion.10
  413.1 2.1 fusion.22
  (88 shorter events, 22.5 us)
Async XLA Ops:
  0.0 357.5 %copy-start = (bf16[640,1920]{1,0:T(8,128)(2,1)S(1)}, bf16[640,1920]{1,0:T(8,128)(2,1)}, u32[]{:S(2)}) copy-start(bf16[640,1920]{1,0:T(8,128)(2,1)} %param.19) | copy-start | bytes 7372804
  17.6 15.4 %copy-start.1 = (bf16[8,1,16,640]{3,2,1,0:T(8,128)(2,1)S(1)}, bf16[8,1,16,640]{3,2,1,0:T(8,128)(2,1)}, u32[]{:S(2)}) copy-start(bf16[8,1,16,640]{3,2,1,0:T(8,128)(2,1)} %param.11) | copy-start | bytes 491524
  17.6 334.5 %all-to-all-start = ((bf16[16,360,640]{2,1,0:T(8,128)(2,1)}), bf16[16,360,640]{2,1,0:T(8,128)(2,1)}, u32[]{:S(2)}, u32[]{:S(2)}) async-start(bf16[16,360,640]{2,1,0:T(8,128)(2,1)} %stack.2), calls=%async_computation | async-start | bytes 14745600 | tf_op jit(solution)/shard_map/all_to_all | solution.py:61
  33.0 29.3 %copy-start.5 = (f32[640]{0:T(1024)S(1)}, f32[640]{0:T(1024)}, u32[]{:S(2)}) copy-start(f32[640]{0:T(1024)} %param.14) | copy-start | bytes 7684
  33.0 29.3 %copy-start.6 = (f32[640]{0:T(1024)S(1)}, f32[640]{0:T(1024)}, u32[]{:S(2)}) copy-start(f32[640]{0:T(1024)} %param.13) | copy-start | bytes 7684
  33.0 32.1 %copy-start.11 = (s32[28]{0:T(128)S(1)}, s32[28]{0:T(128)}, u32[]{:S(2)}) copy-start(s32[28]{0:T(128)} %param.12) | copy-start | bytes 340
  62.4 3.2 collective-permute-start
  63.8 3.3 collective-permute-start.1
  67.4 284.7 %copy-start.7 = (f32[640]{0:T(1024)S(1)}, f32[640]{0:T(1024)}, u32[]{:S(2)}) copy-start(f32[640]{0:T(1024)} %param.16) | copy-start | bytes 7684
  352.1 5.3 %copy-start.8 = (f32[640]{0:T(1024)S(1)}, f32[640]{0:T(1024)}, u32[]{:S(2)}) copy-start(f32[640]{0:T(1024)} %param.18) | copy-start | bytes 7684
  352.1 5.3 %copy-start.9 = (f32[640]{0:T(1024)S(1)}, f32[640]{0:T(1024)}, u32[]{:S(2)}) copy-start(f32[640]{0:T(1024)} %param.17) | copy-start | bytes 7684
  358.8 18.1 %collective-permute-start.6 = (bf16[8,16,640]{2,1,0:T(8,128)(2,1)}, bf16[8,16,640]{2,1,0:T(8,128)(2,1)}, u32[]{:S(2)}, u32[]{:S(2)}) collective-permute-start(bf16[8,16,640]{2,1,0:T(8,128)(2,1)} %get-tuple-element.11), channel_id=1, source_target_pairs={{0,16},{8,24},{16,32},{24,40},{32,48},{40,56},{48,64},{56,72},{64,... | collective-permute-start | bytes 491528 | tf_op jit(solution)/shard_map/ppermute | solution.py:16
  364.0 15.2 %collective-permute-start.2 = (bf16[8,16,640]{2,1,0:T(8,128)(2,1)S(1)}, bf16[8,16,640]{2,1,0:T(8,128)(2,1)S(1)}, u32[]{:S(2)}, u32[]{:S(2)}) collective-permute-start(bf16[8,16,640]{2,1,0:T(8,128)(2,1)S(1)} %get-tuple-element.10), channel_id=1, source_target_pairs={{0,16},{8,24},{16,32},{24,40},{32,48},{40,56},{48,64},{56,72},{64,... | collective-permute-start | bytes 491528 | tf_op jit(solution)/shard_map/ppermute | solution.py:16
  368.7 12.4 %collective-permute-start.7 = (bf16[8,16,640]{2,1,0:T(8,128)(2,1)}, bf16[8,16,640]{2,1,0:T(8,128)(2,1)S(1)}, u32[]{:S(2)}, u32[]{:S(2)}) collective-permute-start(bf16[8,16,640]{2,1,0:T(8,128)(2,1)} %get-tuple-element.11), channel_id=1, source_target_pairs={{0,8},{8,16},{16,24},{24,32},{32,40},{40,48},{48,56},{56,64},{64,7... | collective-permute-start | bytes 491528 | tf_op jit(solution)/shard_map/ppermute | solution.py:16
  372.3 10.4 %collective-permute-start.3 = (bf16[8,16,640]{2,1,0:T(8,128)(2,1)S(1)}, bf16[8,16,640]{2,1,0:T(8,128)(2,1)S(1)}, u32[]{:S(2)}, u32[]{:S(2)}) collective-permute-start(bf16[8,16,640]{2,1,0:T(8,128)(2,1)S(1)} %get-tuple-element.10), channel_id=1, source_target_pairs={{0,8},{8,16},{16,24},{24,32},{32,40},{40,48},{48,56},{56,64},{64,7... | collective-permute-start | bytes 491528 | tf_op jit(solution)/shard_map/ppermute | solution.py:16
  375.6 9.4 %collective-permute-start.4 = (bf16[8,16,640]{2,1,0:T(8,128)(2,1)S(1)}, bf16[8,16,640]{2,1,0:T(8,128)(2,1)S(1)}, u32[]{:S(2)}, u32[]{:S(2)}) collective-permute-start(bf16[8,16,640]{2,1,0:T(8,128)(2,1)S(1)} %get-tuple-element.10), channel_id=1, source_target_pairs={{8,0},{16,8},{24,16},{32,24},{40,32},{48,40},{56,48},{64,56},{72,6... | collective-permute-start | bytes 491528 | tf_op jit(solution)/shard_map/ppermute | solution.py:16
  376.9 16.5 %collective-permute-start.5 = (bf16[8,16,640]{2,1,0:T(8,128)(2,1)S(1)}, bf16[8,16,640]{2,1,0:T(8,128)(2,1)S(1)}, u32[]{:S(2)}, u32[]{:S(2)}) collective-permute-start(bf16[8,16,640]{2,1,0:T(8,128)(2,1)S(1)} %get-tuple-element.10), channel_id=1, source_target_pairs={{16,0},{24,8},{32,16},{40,24},{48,32},{56,40},{64,48},{72,56},{80,... | collective-permute-start | bytes 491528 | tf_op jit(solution)/shard_map/ppermute | solution.py:16
  379.2 19.1 %collective-permute-start.8 = (bf16[8,16,640]{2,1,0:T(8,128)(2,1)}, bf16[8,16,640]{2,1,0:T(8,128)(2,1)}, u32[]{:S(2)}, u32[]{:S(2)}) collective-permute-start(bf16[8,16,640]{2,1,0:T(8,128)(2,1)} %get-tuple-element.11), channel_id=1, source_target_pairs={{8,0},{16,8},{24,16},{32,24},{40,32},{48,40},{56,48},{64,56},{72,6... | collective-permute-start | bytes 491528 | tf_op jit(solution)/shard_map/ppermute | solution.py:16
  381.2 21.0 %collective-permute-start.9 = (bf16[8,16,640]{2,1,0:T(8,128)(2,1)}, bf16[8,16,640]{2,1,0:T(8,128)(2,1)}, u32[]{:S(2)}, u32[]{:S(2)}) collective-permute-start(bf16[8,16,640]{2,1,0:T(8,128)(2,1)} %get-tuple-element.11), channel_id=1, source_target_pairs={{16,0},{24,8},{32,16},{40,24},{48,32},{56,40},{64,48},{72,56},{80,... | collective-permute-start | bytes 491528 | tf_op jit(solution)/shard_map/ppermute | solution.py:16
  384.1 0.9 copy-start.3
  394.1 4.2 %copy-start.4 = (bf16[40,16,640]{2,1,0:T(8,128)(2,1)S(1)}, bf16[40,16,640]{2,1,0:T(8,128)(2,1)}, u32[]{:S(2)}) copy-start(bf16[40,16,640]{2,1,0:T(8,128)(2,1)} %copy-done.3) | copy-start | bytes 2457604
  409.9 1.8 copy-start.2
  411.6 1.5 copy-start.10
